TPU v7x, 128 devices: a whole 4x4x4 slice. The times are simulated.
128 devices in a mesh: dp: 4 (over z), fsdp: 32 (over y, x, core).
Axes of the slice: x: 4, y: 4, z: 4, core: 2. Of those that a mesh axis runs over, the one named last changes fastest.
Arguments:
- logged: bfloat16 [2048, 8192], P('dp', 'fsdp'), may hold values from -6 to 6
- pairs: int32 [512, 2], P('dp'), may hold values from 0 to 511
- clicks: int32 [512], P('dp'), may hold values 0 or 1
- query_pairs: int32 [32, 2], P('dp'), may hold values from 0 to 511
- query_clicks: int32 [32], P('dp'), may hold values 0 or 1
- first_weight: bfloat16 [8192, 8192], P(None, 'fsdp'), may hold values from -0.0625 to 0.0625
- second_weight: bfloat16 [8192, 8192], P(None, 'fsdp'), may hold values from -0.0625 to 0.0625
- head_weight: float32 [8192], P('fsdp'), may hold values from -0.0625 to 0.0625
Outputs:
- solution: float32 [8192, 8192], P('dp', 'fsdp')
- influence: float32 [512], P('dp')
Inputs may be any that keep to these rules, and one draw needn't show every extreme that they name: Each block of 128 pairs indexes rows within the matching block of 512 logged rows. `query_pairs`: each block of 8 query pairs indexes rows within the matching block of 512 logged rows.
All inputs are finite; a program needn't handle non-finite values. No bound on the sum of `clicks` or of `query_clicks` on one device may be relied on, other than what follows from the above.
Results may differ from a plain program's by a relative error of at most 0.035.
Values may be sent and summed in bfloat16 or wider, within the bound.
A program may use at most 128 MiB of HBM per device.

v0:
```python
import jax
import jax.numpy as jnp
from jax import lax
from jax.sharding import PartitionSpec as P

DAMPING = 0.01


def pair_terms(first_score, second_score, outcome):
    signed = 2.0 * outcome.astype(jnp.float32) - 1.0
    margin = first_score - second_score
    slope_term = -signed * jax.nn.sigmoid(-signed * margin)
    curve_term = jax.nn.sigmoid(signed * margin) * jax.nn.sigmoid(-signed * margin)
    return (slope_term, curve_term)


def solver_total(value):
    return lax.psum(value, ("dp", "fsdp"))


def contract_rows(left, right):
    return lax.dot_general(
        left, right, (((0,), (0,)), ((), ())), preferred_element_type=jnp.float32
    )


def local(
    logged, pairs, clicks, query_pairs, query_clicks, first_weight, second_weight, head_weight
):
    npairs = pairs.shape[0]
    nqueries = query_pairs.shape[0]
    count = 2 * npairs
    row_ids = jnp.concatenate([pairs[:, 0], pairs[:, 1], query_pairs[:, 0], query_pairs[:, 1]])
    local_rows = jnp.take(logged, row_ids, axis=0)
    feats = lax.all_gather(local_rows, "fsdp", axis=1, tiled=True)
    hidden = jnp.tanh(jnp.dot(feats, first_weight, preferred_element_type=jnp.float32)).astype(
        jnp.bfloat16
    )
    second_pre = jnp.dot(
        lax.all_gather(hidden, "fsdp", axis=1, tiled=True),
        second_weight,
        preferred_element_type=jnp.float32,
    )
    output_act = jnp.tanh(second_pre)
    scores_all = lax.psum(jnp.sum(output_act * head_weight, axis=1), "fsdp")
    coef = (head_weight * (1.0 - output_act * output_act)).astype(jnp.bfloat16)
    back_term = lax.dot_general(
        coef, second_weight, (((1,), (1,)), ((), ())), preferred_element_type=jnp.float32
    )
    back = lax.psum_scatter(
        back_term.astype(jnp.bfloat16), "fsdp", scatter_dimension=1, tiled=True
    ).astype(jnp.float32)
    hidden_float = hidden.astype(jnp.float32)
    mixing = (1.0 - hidden_float * hidden_float) * back
    slope_train, curve_train = pair_terms(scores_all[:npairs], scores_all[npairs:count], clicks)
    slope_query = pair_terms(
        scores_all[count : count + nqueries], scores_all[count + nqueries :], query_clicks
    )[0]
    query_err = jnp.concatenate([slope_query, -slope_query])
    query_rows = (query_err[:, None] * mixing[count:]).astype(jnp.bfloat16)
    grad_local = contract_rows(feats[count:], query_rows)
    gradient = lax.psum_scatter(
        grad_local.astype(jnp.bfloat16), "dp", scatter_dimension=0, tiled=True
    ).astype(jnp.float32)
    train_feats = feats[:count]
    train_mix = mixing[:count]

    def apply_curvature(direction):
        packed = direction.astype(jnp.bfloat16)
        gathered = lax.all_gather(packed, "dp", axis=0, tiled=True)
        project = jnp.dot(train_feats, gathered, preferred_element_type=jnp.float32)
        response = lax.psum(jnp.sum(train_mix * project, axis=1), "fsdp")
        rdiff = response[:npairs] - response[npairs:]
        resp_err = jnp.concatenate([curve_train * rdiff, -curve_train * rdiff])
        resp_rows = (resp_err[:, None] * train_mix).astype(jnp.bfloat16)
        term = contract_rows(train_feats, resp_rows)
        return (packed, gathered, term, rdiff)

    norm_first = solver_total(jnp.sum(gradient * gradient))
    packed_first, gathered_first, local_first, rdiff_first = apply_curvature(gradient)
    product_first = lax.psum_scatter(
        local_first.astype(jnp.bfloat16), "dp", scatter_dimension=0, tiled=True
    ).astype(jnp.float32)
    curv_first = (
        solver_total(jnp.sum(packed_first.astype(jnp.float32) * product_first))
        + DAMPING * norm_first
    )
    alpha_first = norm_first / curv_first
    residual_next = gradient - alpha_first * (product_first + DAMPING * gradient)
    norm_next = solver_total(jnp.sum(residual_next * residual_next))
    direction_next = residual_next + norm_next / norm_first * gradient
    packed_next, gathered_next, local_next, rdiff_next = apply_curvature(direction_next)
    damped_part = DAMPING * jnp.sum(direction_next * direction_next)
    product_next = lax.psum_scatter(
        local_next.astype(jnp.bfloat16), "dp", scatter_dimension=0, tiled=True
    ).astype(jnp.float32)
    inner_part = jnp.sum(packed_next.astype(jnp.float32) * product_next) + damped_part
    curv_next = solver_total(inner_part)
    alpha_next = norm_next / curv_next
    solution = alpha_first * gradient + alpha_next * direction_next
    influence = -slope_train * (alpha_first * rdiff_first + alpha_next * rdiff_next)
    return (solution, influence)


def solution(mesh):
    placed = (
        P("dp", "fsdp"),
        P("dp", None),
        P("dp"),
        P("dp", None),
        P("dp"),
        P(None, "fsdp"),
        P(None, "fsdp"),
        P("fsdp"),
    )
    return jax.shard_map(
        local, mesh=mesh, in_specs=placed, out_specs=(P("dp", "fsdp"), P("dp")), check_vma=False
    )
```

profile of v0, /device:TPU:1, one launch (start us, length us, event | category | flops | bytes accessed | tf_op | source)
XLA Modules:
  0.0 815.9 jit_solution(4647815058639752397)
XLA Ops:
  7.2 0.0 copy-start
  7.2 0.0 all-gather.5.cloned.1.call-start
  7.2 0.8 slice_bitcast_fusion.3
  8.0 0.8 slice_bitcast_fusion.1
  8.7 0.1 fusion.33
  8.8 0.0 copy-done
  8.8 2.0 gather_fusion
  10.8 0.1 compare_and_fusion
  10.9 0.8 broadcast_select_fusion
  11.7 0.0 all-gather.5.cloned.1.call-update
  11.7 0.0 copy-start.6
  11.7 0.0 all-gather.7.cloned.1.call-start
  11.8 53.5 %all-gather.5.cloned.1.call-done = bf16[272,8192]{1,0:T(8,128)(2,1)} async-done(((bf16[272,256]{1,0:T(8,128)(2,1)}), bf16[272,8192]{1,0:T(8,128)(2,1)}) %all-gather.5.cloned.1.call-update) | async-done | bytes 4456464 | tf_op jit(solution)/shard_map/all_gather | solution.py:35
  65.2 5.5 fusion.17
  70.8 0.0 all-gather.7.cloned.1.call-update
  70.8 0.0 reduce-scatter.5.cloned.1.call-start
  70.8 49.4 %all-gather.7.cloned.1.call-done = bf16[272,8192]{1,0:T(8,128)(2,1)} async-done(((bf16[272,256]{1,0:T(8,128)(2,1)}), bf16[272,8192]{1,0:T(8,128)(2,1)}) %all-gather.7.cloned.1.call-update) | async-done | bytes 4456464 | tf_op jit(solution)/shard_map/all_gather | solution.py:40
  120.2 0.0 copy-done.6
  120.2 5.1 multiply_reduce_fusion.3
  125.4 0.0 copy-done.4
  125.4 3.5 convolution_convert_fusion
  128.8 0.0 reduce-scatter.5.cloned.1.call-update
  128.8 0.0 reduce-scatter.7.cloned.1.call-start
  128.9 62.7 %psum.49 = f32[272]{0:T(512)S(1)} all-reduce(f32[272]{0:T(512)S(1)} %get-tuple-element.23), channel_id=1, replica_groups=mesh['dp'=4,'fsdp'=32] {'fsdp'}, use_global_device_ids=true, to_apply=%region_1.2 | all-reduce | flops 272 | bytes 2176 | tf_op jit(solution)/shard_map/psum | solution.py:45
  191.6 0.0 copy-done.8
  191.6 0.1 fusion.37
  191.7 0.1 pad_maximum_fusion.2
  191.7 18.3 %reduce-scatter.5.cloned.1.call-done = bf16[272,256]{1,0:T(8,128)(2,1)} async-done(((bf16[272,8192]{1,0:T(8,128)(2,1)}), bf16[272,256]{1,0:T(8,128)(2,1)}) %reduce-scatter.5.cloned.1.call-update) | async-done | bytes 139280 | tf_op jit(solution)/shard_map/reduce_scatter | solution.py:50
  210.1 0.0 copy-done.5
  210.1 1.0 convert_multiply_fusion.5
  211.0 4.2 convolution_convert_fusion.3
  215.3 0.0 reduce-scatter.7.cloned.1.call-update
  215.3 0.0 all-gather.9.cloned.1.call-start
  215.3 48.5 %reduce-scatter.7.cloned.1.call-done = bf16[2048,256]{1,0:T(8,128)(2,1)} async-done(((bf16[8192,256]{1,0:T(8,128)(2,1)}), bf16[2048,256]{1,0:T(8,128)(2,1)}) %reduce-scatter.7.cloned.1.call-update) | async-done | bytes 1048592 | tf_op jit(solution)/shard_map/reduce_scatter | solution.py:62
  263.8 0.0 all-gather.9.cloned.1.call-update
  263.9 0.0 copy-start.7
  263.9 0.0 reduce-scatter.9.cloned.1.call-start
  263.9 49.5 %all-gather.9.cloned.1.call-done = bf16[8192,256]{1,0:T(8,128)(2,1)} async-done(((bf16[2048,256]{1,0:T(8,128)(2,1)}), bf16[8192,256]{1,0:T(8,128)(2,1)}) %all-gather.9.cloned.1.call-update) | async-done | bytes 4194320 | tf_op jit(solution)/shard_map/all_gather | solution.py:70
  313.4 4.8 fusion.22
  318.2 62.7 %psum.51 = f32[256]{0:T(256)S(1)} all-reduce(f32[256]{0:T(256)S(1)} %fusion.22), channel_id=1, replica_groups=mesh['dp'=4,'fsdp'=32] {'fsdp'}, use_global_device_ids=true, to_apply=%region_7.8 | all-reduce | flops 256 | bytes 2048 | tf_op jit(solution)/shard_map/psum | solution.py:72
  380.9 0.0 copy-done.7
  380.9 5.5 convolution_convert_fusion.2
  386.4 0.0 reduce-scatter.9.cloned.1.call-update
  386.5 0.0 all-gather.11.cloned.1.call-start
  386.5 46.8 %reduce-scatter.9.cloned.1.call-done = bf16[2048,256]{1,0:T(8,128)(2,1)} async-done(((bf16[8192,256]{1,0:T(8,128)(2,1)}), bf16[2048,256]{1,0:T(8,128)(2,1)}) %reduce-scatter.9.cloned.1.call-update) | async-done | bytes 1048592 | tf_op jit(solution)/shard_map/reduce_scatter | solution.py:81
  433.3 0.0 copy-done.1
  433.3 2.5 fusion.8
  435.8 64.6 %all-reduce = (f32[]{:T(128)}, f32[]{:T(128)}) all-reduce(f32[]{:T(128)} %get-tuple-element.3, f32[]{:T(128)} %get-tuple-element.2), channel_id=1, replica_groups=mesh['dp'=4,'fsdp'=32] {'dp','fsdp'}, use_global_device_ids=true, to_apply=%region_5.6 | all-reduce | flops 2 | bytes 16 | tf_op jit(solution)/shard_map/psum | solution.py:18
  502.3 2.4 multiply_reduce_fusion.2
  504.7 64.3 %psum.53 = f32[]{:T(128)} all-reduce(f32[]{:T(128)} %multiply_reduce_fusion.2), channel_id=1, replica_groups=mesh['dp'=4,'fsdp'=32] {'dp','fsdp'}, use_global_device_ids=true, to_apply=%region_12.13 | all-reduce | flops 1 | bytes 8 | tf_op jit(solution)/shard_map/psum | solution.py:18
  570.4 0.0 copy-done.2
  570.4 2.3 multiply_reduce_fusion
  572.7 0.0 all-gather.11.cloned.1.call-update
  572.7 0.0 reduce-scatter.11.cloned.1.call-start
  572.7 45.0 %all-gather.11.cloned.1.call-done = bf16[8192,256]{1,0:T(8,128)(2,1)} async-done(((bf16[2048,256]{1,0:T(8,128)(2,1)}), bf16[8192,256]{1,0:T(8,128)(2,1)}) %all-gather.11.cloned.1.call-update) | async-done | bytes 4194320 | tf_op jit(solution)/shard_map/all_gather | solution.py:70
  617.7 4.8 fusion.19
  622.5 62.7 %psum.54 = f32[256]{0:T(256)S(1)} all-reduce(f32[256]{0:T(256)S(1)} %fusion.19), channel_id=1, replica_groups=mesh['dp'=4,'fsdp'=32] {'fsdp'}, use_global_device_ids=true, to_apply=%region_14.15 | all-reduce | flops 256 | bytes 2048 | tf_op jit(solution)/shard_map/psum | solution.py:72
  685.2 5.5 convolution_convert_fusion.1
  690.7 0.0 reduce-scatter.11.cloned.1.call-update
  691.5 46.1 %reduce-scatter.11.cloned.1.call-done = bf16[2048,256]{1,0:T(8,128)(2,1)} async-done(((bf16[8192,256]{1,0:T(8,128)(2,1)}), bf16[2048,256]{1,0:T(8,128)(2,1)}) %reduce-scatter.11.cloned.1.call-update) | async-done | bytes 1048592 | tf_op jit(solution)/shard_map/reduce_scatter | solution.py:94
  737.6 2.4 multiply_reduce_fusion.1
  740.6 64.5 %psum.55 = f32[]{:T(128)} all-reduce(f32[]{:T(128)S(6)} %add.83), channel_id=1, replica_groups=mesh['dp'=4,'fsdp'=32] {'dp','fsdp'}, use_global_device_ids=true, to_apply=%region_18.19 | all-reduce | flops 1 | bytes 8 | tf_op jit(solution)/shard_map/psum | solution.py:18
  806.5 0.5 add_multiply_fusion
  807.0 2.1 fusion.9
  (13 shorter events, 0.1 us)
Async XLA Ops:
  7.2 1.7 copy-start
  7.2 58.0 %all-gather.5.cloned.1.call-start = ((), (), s32[]{:S(2)}) async-start(), calls=%async_computation.4 | async-start | bytes 4595712 | tf_op jit(solution)/shard_map/all_gather | solution.py:35
  11.7 108.5 %copy-start.6 = (f32[256]{0:T(256)S(1)}, f32[256]{0:T(256)}, u32[]{:S(2)}) copy-start(f32[256]{0:T(256)} %param.15) | copy-start | bytes 3076
  11.7 108.5 %all-gather.7.cloned.1.call-start = ((), (), s32[]{:S(2)}) async-start(), calls=%async_computation.5 | async-start | bytes 4595712 | tf_op jit(solution)/shard_map/all_gather | solution.py:40
  70.8 139.3 %reduce-scatter.5.cloned.1.call-start = ((), (), s32[]{:S(2)}) async-start(), calls=%async_computation.6 | async-start | bytes 4595712 | tf_op jit(solution)/shard_map/reduce_scatter | solution.py:50
  120.2 5.1 copy-start.4
  128.8 62.8 %copy-start.8 = (s32[8]{0:T(128)S(1)}, s32[8]{0:T(128)}, u32[]{:S(2)}) copy-start(s32[8]{0:T(128)} %param.12) | copy-start | bytes 100
  128.8 81.3 %copy-start.5 = (bf16[272,256]{1,0:T(8,128)(2,1)S(1)}, bf16[272,256]{1,0:T(8,128)(2,1)}, u32[]{:S(2)}) copy-start(bf16[272,256]{1,0:T(8,128)(2,1)} %fusion.17) | copy-start | bytes 417796
  128.8 135.0 %reduce-scatter.7.cloned.1.call-start = ((), (), s32[]{:S(2)}) async-start(), calls=%async_computation.7 | async-start | bytes 5242880 | tf_op jit(solution)/shard_map/reduce_scatter | solution.py:62
  215.3 98.1 %all-gather.9.cloned.1.call-start = ((), (), s32[]{:S(2)}) async-start(), calls=%async_computation.8 | async-start | bytes 5242880 | tf_op jit(solution)/shard_map/all_gather | solution.py:70
  263.9 117.0 %copy-start.7 = (s32[128]{0:T(128)S(1)}, s32[128]{0:T(128)}, u32[]{:S(2)}) copy-start(s32[128]{0:T(128)} %param.10) | copy-start | bytes 1540
  263.9 169.4 %reduce-scatter.9.cloned.1.call-start = ((), (), s32[]{:S(2)}) async-start(), calls=%async_computation.9 | async-start | bytes 5242880 | tf_op jit(solution)/shard_map/reduce_scatter | solution.py:81
  386.4 46.9 %copy-start.1 = (bf16[2048,256]{1,0:T(8,128)(2,1)S(1)}, bf16[2048,256]{1,0:T(8,128)(2,1)}, u32[]{:S(2)}) copy-start(bf16[2048,256]{1,0:T(8,128)(2,1)} %reduce-scatter.7.cloned.1.call-done) | copy-start | bytes 3145732
  386.5 231.2 %all-gather.11.cloned.1.call-start = ((), (), s32[]{:S(2)}) async-start(), calls=%async_computation.10 | async-start | bytes 5242880 | tf_op jit(solution)/shard_map/all_gather | solution.py:70
  433.3 137.1 %copy-start.2 = (bf16[2048,256]{1,0:T(8,128)(2,1)S(1)}, bf16[2048,256]{1,0:T(8,128)(2,1)}, u32[]{:S(2)}) copy-start(bf16[2048,256]{1,0:T(8,128)(2,1)} %reduce-scatter.9.cloned.1.call-done) | copy-start | bytes 3145732
  572.7 164.9 %reduce-scatter.11.cloned.1.call-start = ((), (), s32[]{:S(2)}) async-start(), calls=%async_computation.11 | async-start | bytes 5242880 | tf_op jit(solution)/shard_map/reduce_scatter | solution.py:94
  690.7 46.9 %copy-start.3 = (bf16[2048,256]{1,0:T(8,128)(2,1)S(1)}, bf16[2048,256]{1,0:T(8,128)(2,1)}, u32[]{:S(2)}) copy-start(bf16[2048,256]{1,0:T(8,128)(2,1)} %get-tuple-element.12) | copy-start | bytes 3145732
Sparse Core Ops, SparseCore 0:
  11.8 53.3 all-gather.4
  70.9 49.2 all-gather.6
  129.0 81.0 reduce-scatter.4
  215.4 48.3 reduce-scatter.6
  265.4 47.9 all-gather.8
  386.6 46.6 reduce-scatter.8
  572.8 44.8 all-gather.10
  690.9 46.6 reduce-scatter.10
where the time goes:
time: 817 us; the launch traced here: 816 us
  blocking collectives  381 us (47%)
  waiting for transfers between devices  357 us (44%)
  matrix products  38.9 us (5%)
  between operations  20.2 us (2%)
  other arithmetic  14.2 us (2%)
    psum x3, blocking collectives, solver_total(): return lax.psum(value, ('dp', 'fsdp'))  193 us
    psum x2, blocking collectives, apply_curvature(): response = lax.psum(jnp.sum(train_mix * project, axis=1), 'fsdp')  125 us
    all_gather x2, waiting for transfers between devices, apply_curvature(): gathered = lax.all_gather(packed, 'dp', axis=0, tiled=True)  94.4 us
    psum x1, blocking collectives, local(): scores_all = lax.psum(jnp.sum(output_act * head_weight, axis=1), 'fsdp')  62.7 us
    all_gather x1, waiting for transfers between devices, local(): feats = lax.all_gather(local_rows, 'fsdp', axis=1, tiled=True)  53.5 us
    all_gather x1, waiting for transfers between devices, local(): lax.all_gather(hidden, 'fsdp', axis=1, tiled=True)  49.4 us
    reduce_scatter x1, waiting for transfers between devices, local(): lax.psum_scatter(grad_local.astype(jnp.bfloat16), 'dp', scatter_dimension...  48.5 us
    reduce_scatter x1, waiting for transfers between devices, local(): lax.psum_scatter(local_first.astype(jnp.bfloat16), 'dp', scatter_dimensio...  46.8 us
  transfers between devices with their start and end apart: 8, of which 8 were waited for; matrix products, arithmetic and copies ran while one was open for 0% of the time, Pallas kernels for 0%

commit v1 on v0

--- a/solution.py
+++ b/solution.py
@@ -15,7 +15,7 @@
 
 
 def solver_total(value):
-    return lax.psum(value, ("dp", "fsdp"))
+    return lax.psum(lax.psum(value, "fsdp"), "dp")
 
 
 def contract_rows(left, right):

time: 817 us -> 846 us (1.035)
  blocking collectives: 381 us -> 406 us
    psum x3 -> x6, blocking collectives: 193 us -> 218 us  [solver_total(): return lax.psum(lax.psum(value, 'fsdp'), 'dp')]
where the time goes in v1:
time: 846 us; the launch traced here: 840 us
  blocking collectives  406 us (48%)
  waiting for transfers between devices  357 us (42%)
  matrix products  38.9 us (5%)
  between operations  20.2 us (2%)
  other arithmetic  14.2 us (2%)
    psum x6, blocking collectives, solver_total(): return lax.psum(lax.psum(value, 'fsdp'), 'dp')  218 us
    psum x2, blocking collectives, apply_curvature(): response = lax.psum(jnp.sum(train_mix * project, axis=1), 'fsdp')  125 us
    all_gather x2, waiting for transfers between devices, apply_curvature(): gathered = lax.all_gather(packed, 'dp', axis=0, tiled=True)  94 us
    psum x1, blocking collectives, local(): scores_all = lax.psum(jnp.sum(output_act * head_weight, axis=1), 'fsdp')  62.7 us
    all_gather x1, waiting for transfers between devices, local(): feats = lax.all_gather(local_rows, 'fsdp', axis=1, tiled=True)  53.5 us
    all_gather x1, waiting for transfers between devices, local(): lax.all_gather(hidden, 'fsdp', axis=1, tiled=True)  49.4 us
    reduce_scatter x1, waiting for transfers between devices, local(): lax.psum_scatter(grad_local.astype(jnp.bfloat16), 'dp', scatter_dimension...  48.5 us
    reduce_scatter x1, waiting for transfers between devices, local(): lax.psum_scatter(local_first.astype(jnp.bfloat16), 'dp', scatter_dimensio...  46.8 us
  transfers between devices with their start and end apart: 8, of which 8 were waited for; matrix products, arithmetic and copies ran while one was open for 0% of the time, Pallas kernels for 0%

profile of v1, /device:TPU:1, one launch (start us, length us, event | category | flops | bytes accessed | tf_op | source)
XLA Modules:
  0.0 840.0 jit_solution(17097973850317161130)
XLA Ops:
  7.2 0.0 copy-start
  7.2 0.0 all-gather.5.cloned.1.call-start
  7.2 0.8 slice_bitcast_fusion.3
  8.0 0.8 slice_bitcast_fusion.1
  8.7 0.1 fusion.33
  8.8 0.0 copy-done
  8.8 2.0 gather_fusion
  10.8 0.1 compare_and_fusion
  10.9 0.8 broadcast_select_fusion
  11.7 0.0 all-gather.5.cloned.1.call-update
  11.7 0.0 copy-start.6
  11.7 0.0 all-gather.7.cloned.1.call-start
  11.8 53.5 %all-gather.5.cloned.1.call-done = bf16[272,8192]{1,0:T(8,128)(2,1)} async-done(((bf16[272,256]{1,0:T(8,128)(2,1)}), bf16[272,8192]{1,0:T(8,128)(2,1)}) %all-gather.5.cloned.1.call-update) | async-done | bytes 4456464 | tf_op jit(solution)/shard_map/all_gather | solution.py:35
  65.2 5.5 fusion.17
  70.8 0.0 all-gather.7.cloned.1.call-update
  70.8 0.0 reduce-scatter.5.cloned.1.call-start
  70.8 49.4 %all-gather.7.cloned.1.call-done = bf16[272,8192]{1,0:T(8,128)(2,1)} async-done(((bf16[272,256]{1,0:T(8,128)(2,1)}), bf16[272,8192]{1,0:T(8,128)(2,1)}) %all-gather.7.cloned.1.call-update) | async-done | bytes 4456464 | tf_op jit(solution)/shard_map/all_gather | solution.py:40
  120.2 0.0 copy-done.6
  120.2 5.1 multiply_reduce_fusion.3
  125.4 0.0 copy-done.4
  125.4 3.5 convolution_convert_fusion
  128.8 0.0 reduce-scatter.5.cloned.1.call-update
  128.8 0.0 reduce-scatter.7.cloned.1.call-start
  128.9 62.7 %psum.77 = f32[272]{0:T(512)S(1)} all-reduce(f32[272]{0:T(512)S(1)} %get-tuple-element.25), channel_id=1, replica_groups=mesh['dp'=4,'fsdp'=32] {'fsdp'}, use_global_device_ids=true, to_apply=%region_1.2 | all-reduce | flops 272 | bytes 2176 | tf_op jit(solution)/shard_map/psum | solution.py:45
  191.6 0.0 copy-done.8
  191.6 0.1 fusion.37
  191.7 0.1 pad_maximum_fusion.2
  191.7 18.3 %reduce-scatter.5.cloned.1.call-done = bf16[272,256]{1,0:T(8,128)(2,1)} async-done(((bf16[272,8192]{1,0:T(8,128)(2,1)}), bf16[272,256]{1,0:T(8,128)(2,1)}) %reduce-scatter.5.cloned.1.call-update) | async-done | bytes 139280 | tf_op jit(solution)/shard_map/reduce_scatter | solution.py:50
  210.1 0.0 copy-done.5
  210.1 1.0 convert_multiply_fusion.5
  211.0 4.2 convolution_convert_fusion.3
  215.3 0.0 reduce-scatter.7.cloned.1.call-update
  215.3 0.0 all-gather.9.cloned.1.call-start
  215.3 48.5 %reduce-scatter.7.cloned.1.call-done = bf16[2048,256]{1,0:T(8,128)(2,1)} async-done(((bf16[8192,256]{1,0:T(8,128)(2,1)}), bf16[2048,256]{1,0:T(8,128)(2,1)}) %reduce-scatter.7.cloned.1.call-update) | async-done | bytes 1048592 | tf_op jit(solution)/shard_map/reduce_scatter | solution.py:62
  263.8 0.0 all-gather.9.cloned.1.call-update
  263.9 0.0 copy-start.7
  263.9 0.0 reduce-scatter.9.cloned.1.call-start
  263.9 49.5 %all-gather.9.cloned.1.call-done = bf16[8192,256]{1,0:T(8,128)(2,1)} async-done(((bf16[2048,256]{1,0:T(8,128)(2,1)}), bf16[8192,256]{1,0:T(8,128)(2,1)}) %all-gather.9.cloned.1.call-update) | async-done | bytes 4194320 | tf_op jit(solution)/shard_map/all_gather | solution.py:70
  313.4 4.8 fusion.22
  318.2 62.7 %psum.80 = f32[256]{0:T(256)S(1)} all-reduce(f32[256]{0:T(256)S(1)} %fusion.22), channel_id=1, replica_groups=mesh['dp'=4,'fsdp'=32] {'fsdp'}, use_global_device_ids=true, to_apply=%region_8.9 | all-reduce | flops 256 | bytes 2048 | tf_op jit(solution)/shard_map/psum | solution.py:72
  380.9 5.5 convolution_convert_fusion.2
  386.4 0.0 reduce-scatter.9.cloned.1.call-update
  386.5 0.0 all-gather.11.cloned.1.call-start
  386.5 46.8 %reduce-scatter.9.cloned.1.call-done = bf16[2048,256]{1,0:T(8,128)(2,1)} async-done(((bf16[8192,256]{1,0:T(8,128)(2,1)}), bf16[2048,256]{1,0:T(8,128)(2,1)}) %reduce-scatter.9.cloned.1.call-update) | async-done | bytes 1048592 | tf_op jit(solution)/shard_map/reduce_scatter | solution.py:81
  433.3 2.5 fusion.8
  435.8 63.3 %all-reduce = (f32[]{:T(128)}, f32[]{:T(128)}) all-reduce(f32[]{:T(128)} %get-tuple-element.3, f32[]{:T(128)} %get-tuple-element.2), channel_id=1, replica_groups=mesh['dp'=4,'fsdp'=32] {'fsdp'}, use_global_device_ids=true, to_apply=%region_5.6 | all-reduce | flops 2 | bytes 16 | tf_op jit(solution)/shard_map/psum | solution.py:18
  499.0 7.1 all-reduce.1
  508.1 2.4 multiply_reduce_fusion.2
  510.4 69.7 %psum.83 = f32[]{:T(128)} all-reduce(f32[]{:T(128)} %multiply_reduce_fusion.2), channel_id=1, replica_groups=mesh['dp'=4,'fsdp'=32] {'fsdp'}, use_global_device_ids=true, to_apply=%region_14.15 | all-reduce | flops 1 | bytes 8 | tf_op jit(solution)/shard_map/psum | solution.py:18
  580.1 7.6 psum.84
  589.0 2.3 multiply_reduce_fusion
  591.3 0.0 all-gather.11.cloned.1.call-update
  591.4 0.2 reduce-scatter.11.cloned.1.call-start
  591.6 44.5 %all-gather.11.cloned.1.call-done = bf16[8192,256]{1,0:T(8,128)(2,1)} async-done(((bf16[2048,256]{1,0:T(8,128)(2,1)}), bf16[8192,256]{1,0:T(8,128)(2,1)}) %all-gather.11.cloned.1.call-update) | async-done | bytes 4194320 | tf_op jit(solution)/shard_map/all_gather | solution.py:70
  636.1 4.8 fusion.19
  640.9 62.7 %psum.85 = f32[256]{0:T(256)S(1)} all-reduce(f32[256]{0:T(256)S(1)} %fusion.19), channel_id=1, replica_groups=mesh['dp'=4,'fsdp'=32] {'fsdp'}, use_global_device_ids=true, to_apply=%region_17.18 | all-reduce | flops 256 | bytes 2048 | tf_op jit(solution)/shard_map/psum | solution.py:72
  703.6 5.5 convolution_convert_fusion.1
  709.1 0.0 reduce-scatter.11.cloned.1.call-update
  709.9 46.1 %reduce-scatter.11.cloned.1.call-done = bf16[2048,256]{1,0:T(8,128)(2,1)} async-done(((bf16[8192,256]{1,0:T(8,128)(2,1)}), bf16[2048,256]{1,0:T(8,128)(2,1)}) %reduce-scatter.11.cloned.1.call-update) | async-done | bytes 1048592 | tf_op jit(solution)/shard_map/reduce_scatter | solution.py:94
  756.0 2.4 multiply_reduce_fusion.1
  759.0 63.2 %psum.86 = f32[]{:T(128)} all-reduce(f32[]{:T(128)S(6)} %add.91), channel_id=1, replica_groups=mesh['dp'=4,'fsdp'=32] {'fsdp'}, use_global_device_ids=true, to_apply=%region_21.22 | all-reduce | flops 1 | bytes 8 | tf_op jit(solution)/shard_map/psum | solution.py:18
  822.2 7.1 psum.87
  830.6 0.5 add_multiply_fusion
  831.1 2.1 fusion.9
  (16 shorter events, 0.1 us)
Async XLA Ops:
  7.2 1.7 copy-start
  7.2 58.0 %all-gather.5.cloned.1.call-start = ((), (), s32[]{:S(2)}) async-start(), calls=%async_computation.4 | async-start | bytes 4595712 | tf_op jit(solution)/shard_map/all_gather | solution.py:35
  11.7 108.5 %copy-start.6 = (f32[256]{0:T(256)S(1)}, f32[256]{0:T(256)}, u32[]{:S(2)}) copy-start(f32[256]{0:T(256)} %param.15) | copy-start | bytes 3076
  11.7 108.5 %all-gather.7.cloned.1.call-start = ((), (), s32[]{:S(2)}) async-start(), calls=%async_computation.5 | async-start | bytes 4595712 | tf_op jit(solution)/shard_map/all_gather | solution.py:40
  70.8 139.3 %reduce-scatter.5.cloned.1.call-start = ((), (), s32[]{:S(2)}) async-start(), calls=%async_computation.6 | async-start | bytes 4595712 | tf_op jit(solution)/shard_map/reduce_scatter | solution.py:50
  120.2 5.1 copy-start.4
  128.8 62.8 %copy-start.8 = (s32[8]{0:T(128)S(1)}, s32[8]{0:T(128)}, u32[]{:S(2)}) copy-start(s32[8]{0:T(128)} %param.12) | copy-start | bytes 100
  128.8 81.3 %copy-start.5 = (bf16[272,256]{1,0:T(8,128)(2,1)S(1)}, bf16[272,256]{1,0:T(8,128)(2,1)}, u32[]{:S(2)}) copy-start(bf16[272,256]{1,0:T(8,128)(2,1)} %fusion.17) | copy-start | bytes 417796
  128.8 135.0 %reduce-scatter.7.cloned.1.call-start = ((), (), s32[]{:S(2)}) async-start(), calls=%async_computation.7 | async-start | bytes 5242880 | tf_op jit(solution)/shard_map/reduce_scatter | solution.py:62
  215.3 98.1 %all-gather.9.cloned.1.call-start = ((), (), s32[]{:S(2)}) async-start(), calls=%async_computation.8 | async-start | bytes 5242880 | tf_op jit(solution)/shard_map/all_gather | solution.py:70
  263.9 117.0 %copy-start.7 = (s32[128]{0:T(128)S(1)}, s32[128]{0:T(128)}, u32[]{:S(2)}) copy-start(s32[128]{0:T(128)} %param.10) | copy-start | bytes 1540
  263.9 169.4 %reduce-scatter.9.cloned.1.call-start = ((), (), s32[]{:S(2)}) async-start(), calls=%async_computation.9 | async-start | bytes 5242880 | tf_op jit(solution)/shard_map/reduce_scatter | solution.py:81
  386.4 46.9 %copy-start.1 = (bf16[2048,256]{1,0:T(8,128)(2,1)S(1)}, bf16[2048,256]{1,0:T(8,128)(2,1)}, u32[]{:S(2)}) copy-start(bf16[2048,256]{1,0:T(8,128)(2,1)} %reduce-scatter.7.cloned.1.call-done) | copy-start | bytes 3145732
  386.5 249.6 %all-gather.11.cloned.1.call-start = ((), (), s32[]{:S(2)}) async-start(), calls=%async_computation.10 | async-start | bytes 5242880 | tf_op jit(solution)/shard_map/all_gather | solution.py:70
  433.3 155.7 %copy-start.2 = (bf16[2048,256]{1,0:T(8,128)(2,1)S(1)}, bf16[2048,256]{1,0:T(8,128)(2,1)}, u32[]{:S(2)}) copy-start(bf16[2048,256]{1,0:T(8,128)(2,1)} %reduce-scatter.9.cloned.1.call-done) | copy-start | bytes 3145732
  591.4 164.6 %reduce-scatter.11.cloned.1.call-start = ((), (), s32[]{:S(2)}) async-start(), calls=%async_computation.11 | async-start | bytes 5242880 | tf_op jit(solution)/shard_map/reduce_scatter | solution.py:94
  709.1 46.8 %copy-start.3 = (bf16[2048,256]{1,0:T(8,128)(2,1)S(1)}, bf16[2048,256]{1,0:T(8,128)(2,1)}, u32[]{:S(2)}) copy-start(bf16[2048,256]{1,0:T(8,128)(2,1)} %get-tuple-element.14) | copy-start | bytes 3145732
Sparse Core Ops, SparseCore 0:
  11.8 53.3 all-gather.4
  70.9 49.2 all-gather.6
  129.0 81.0 reduce-scatter.4
  215.4 48.3 reduce-scatter.6
  265.4 47.9 all-gather.8
  386.6 46.6 reduce-scatter.8
  591.5 44.5 all-gather.10
  709.3 46.6 reduce-scatter.10
